TPU v7x, 256 devices: a whole 4x4x8 slice. The times are simulated.
256 devices in a mesh: pipe: 8 (over x, core), seq: 8 (over z), tensor: 4 (over y).
Axes of the slice: x: 4, y: 4, z: 8, core: 2. Of those that a mesh axis runs over, the one named last changes fastest.
Arguments:
- hidden: bfloat16 [8, 1024, 14336], P('pipe', 'seq', 'tensor'), may hold values from -6 to 6
- down_weight: bfloat16 [8, 14336, 8192], P('pipe', 'tensor', 'seq'), may hold values from -0.046875 to 0.046875
- resid: bfloat16 [1024, 8192], P('tensor', 'seq'), may hold values from -42 to 42
- target: bfloat16 [1024, 8192], P('tensor', 'seq'), may hold values from -6 to 6
- gain: float32 [8192], P('seq'), may hold values from 0.1 to 1.9
- query_left: float32 [8, 8192, 32], P('pipe', 'seq'), may hold values from -0.0625 to 0.0625
- query_right: bfloat16 [8, 14336, 32], P('pipe', 'tensor'), may hold values from -0.046875 to 0.046875
- query_core: float32 [8, 1024], P('pipe'), may hold values from -6 to 6
- eigen: float32 [8, 1024], P('pipe'), may hold values from 0.1 to 10
- lengths: int32 [32], replicated, may hold values from 1 to 256, 1024 in all
Outputs:
- scores: float32 [32], P(('seq', 'tensor'))
All inputs are finite; a program needn't handle non-finite values.
Results may differ from a plain program's by a relative error of at most 0.0006.
Values may be sent and summed in bfloat16 or wider, within the bound.
No kernel may reach another device: no remote copies, remote signals or barrier semaphores. Data moves between devices by JAX's collectives and lax.ppermute only.
A program may use at most 64 MiB of HBM per device.

v0:
```python
import jax
import jax.numpy as jnp
from jax import lax
from jax.sharding import PartitionSpec as P

D = 8192


def per_device(
    hidden, down_weight, resid, target, gain, query_left, query_right, query_core, eigen, lengths
):
    tensor_count = lax.axis_size("tensor")
    gathered = lax.all_gather(hidden[0], "seq", axis=0, tiled=True)
    total_rows = gathered.shape[0]
    block_rows = total_rows // tensor_count
    weight = down_weight[0]
    right_partial = jnp.dot(gathered, query_right[0], preferred_element_type=jnp.float32)
    partial_value = lax.psum_scatter(
        jnp.dot(gathered, weight, preferred_element_type=jnp.float32).astype(jnp.bfloat16),
        "tensor",
        scatter_dimension=0,
        tiled=True,
    ).astype(jnp.float32)
    summed = lax.psum(partial_value, "pipe")
    stream = resid.astype(jnp.float32) + summed
    weighted_target = gain[None, :] * target.astype(jnp.float32)
    square_sum, inner = lax.psum(
        (jnp.sum(stream * stream, axis=1), jnp.sum(weighted_target * stream, axis=1)), "seq"
    )
    root = jnp.sqrt(square_sum / D + 1e-05)
    grad_stream = (
        weighted_target / root[:, None] - stream * (inner / (D * root * root * root))[:, None]
    )
    left_proj = jnp.dot(grad_stream, query_left[0], precision=lax.Precision.HIGHEST)
    right_proj = lax.psum_scatter(right_partial, "tensor", scatter_dimension=0, tiled=True)
    rank_width = left_proj.shape[1]
    outer = (left_proj[:, :, None] * right_proj[:, None, :]).reshape(
        block_rows, rank_width * rank_width
    )
    ends = jnp.cumsum(lengths)
    starts = ends - lengths
    token = lax.axis_index("tensor") * block_rows + jnp.arange(block_rows, dtype=jnp.int32)
    member = ((token[None, :] >= starts[:, None]) & (token[None, :] < ends[:, None])).astype(
        jnp.float32
    )
    partial_cores = jnp.dot(member, outer, precision=lax.Precision.HIGHEST)
    cores = lax.psum_scatter(partial_cores, ("seq", "tensor"), scatter_dimension=0, tiled=True)
    scaled = cores / eigen[0][None, :]
    score_term = jnp.sum(query_core[0][None, :] * scaled, axis=1)
    self_term = jnp.sum(cores * scaled, axis=1)
    score_total, self_total = lax.psum((score_term, self_term), "pipe")
    return score_total / jnp.sqrt(self_total + 1e-06)


def solution(mesh):
    placed = (
        P("pipe", "seq", "tensor"),
        P("pipe", "tensor", "seq"),
        P("tensor", "seq"),
        P("tensor", "seq"),
        P("seq"),
        P("pipe", "seq", None),
        P("pipe", "tensor", None),
        P("pipe", None),
        P("pipe", None),
        P(),
    )
    return jax.shard_map(
        per_device, mesh=mesh, in_specs=placed, out_specs=P(("seq", "tensor")), check_vma=False
    )
```

profile of v0, /device:TPU:1, one launch (start us, length us, event | category | flops | bytes accessed | tf_op | source)
XLA Modules:
  0.0 375.0 jit_solution(16374362809391073880)
XLA Ops:
  6.5 0.0 copy-start
  6.5 0.0 all-gather.3.cloned.1.call-start
  6.5 0.7 all-gather.3.cloned.1.call-update
  7.3 0.0 copy-start.6
  7.3 0.0 reduce-scatter.3.cloned.1.call-start
  7.3 90.0 %all-gather.3.cloned.1.call-done = bf16[1,1024,3584]{2,1,0:T(8,128)(2,1)} async-done(((bf16[1,128,3584]{2,1,0:T(8,128)(2,1)}), bf16[1,1024,3584]{2,1,0:T(8,128)(2,1)}) %all-gather.3.cloned.1.call-update) | async-done | bytes 7340048 | tf_op jit(solution)/shard_map/all_gather | solution.py:13
  97.3 13.3 %fusion.5 = bf16[1024,1024]{1,0:T(8,128)(2,1)} fusion(bf16[1,3584,1024]{2,1,0:T(8,128)(2,1)} %param.11, bf16[1,1024,3584]{2,1,0:T(8,128)(2,1)} %all-gather.3.cloned.1.call-done), kind=kOutput, calls=%fused_computation.5 | convolution fusion | flops 7517241344 | bytes 16777216 | tf_op jit(solution)/shard_map/dot_general | solution.py:19
  110.6 0.0 copy-start.1
  110.6 0.0 copy-start.2
  110.6 0.0 copy-start.3
  110.6 0.0 copy-start.7
  110.6 0.0 reduce-scatter.3.cloned.1.call-update
  110.6 0.0 reduce-scatter.5.cloned.1.call-start
  110.7 0.0 copy-done.6
  110.7 0.1 copy.15
  110.8 0.1 reduce-window.8
  110.8 0.1 reduce.2
  111.0 0.0 copy-done
  111.0 6.0 %fusion.2 = f32[1024,32]{0,1:T(8,128)} fusion(bf16[1,1024,3584]{2,1,0:T(8,128)(2,1)} %all-gather.3.cloned.1.call-done, bf16[1,3584,32]{1,2,0:T(8,128)(2,1)S(1)} %copy-done), kind=kOutput, calls=%fused_computation.2 | convolution fusion | flops 234881024 | bytes 7700480 | tf_op jit(solution)/shard_map/dot_general | solution.py:17
  116.9 0.0 copy-start.8
  116.9 0.0 copy-start.4
  116.9 0.0 copy-start.5
  116.9 0.0 reduce-scatter.5.cloned.1.call-update
  117.0 0.0 all-reduce.6.cloned.1.call-start
  117.0 24.6 %reduce-scatter.3.cloned.1.call-done = bf16[256,1024]{1,0:T(8,128)(2,1)} async-done(((bf16[1024,1024]{1,0:T(8,128)(2,1)}), bf16[256,1024]{1,0:T(8,128)(2,1)}) %reduce-scatter.3.cloned.1.call-update) | async-done | bytes 524304 | tf_op jit(solution)/shard_map/reduce_scatter | solution.py:18
  141.7 50.4 %all-reduce.7 = f32[256,1024]{1,0:T(8,128)S(1)} all-reduce(bf16[256,1024]{1,0:T(8,128)(2,1)} %reduce-scatter.3.cloned.1.call-done), channel_id=1, replica_groups=mesh['pipe'=8,'seq'=8,'tensor'=4] {'pipe'}, use_global_device_ids=true, to_apply=%region_2.0 | all-reduce | flops 262144 | bytes 1572864 | tf_op jit(solution)/shard_map/psum | solution.py:24
  192.1 0.0 copy-done.1
  192.1 0.0 copy-done.2
  192.1 0.0 copy-done.3
  192.1 0.4 multiply_reduce_fusion.1
  192.5 13.7 %all-reduce.1 = (f32[256]{0:T(256)S(1)}, f32[256]{0:T(256)S(1)}) all-reduce(f32[256]{0:T(256)S(1)} %get-tuple-element.6, f32[256]{0:T(256)S(1)} %get-tuple-element.5), channel_id=1, replica_groups=mesh['pipe'=8,'seq'=8,'tensor'=4] {'seq'}, use_global_device_ids=true, to_apply=%region_6.0 | all-reduce | flops 512 | bytes 4096 | tf_op jit(solution)/shard_map/psum | solution.py:27
  206.2 0.0 copy-done.7
  206.2 1.2 fusion.10
  207.4 0.0 reduce-scatter.5.cloned.1.call-done
  207.5 0.9 broadcast_multiply_fusion
  208.3 1.3 fusion.19
  209.6 0.0 all-reduce.6.cloned.1.call-update
  209.7 0.0 copy-done.8
  209.7 0.6 dynamic-slice
  210.3 137.4 %all-reduce.6.cloned.1.call-done = f32[32,1024]{1,0:T(8,128)} async-done(((f32[32,1024]{1,0:T(8,128)}), f32[32,1024]{1,0:T(8,128)}) %all-reduce.6.cloned.1.call-update) | async-done | bytes 131088
  347.7 0.0 copy-done.4
  347.7 0.0 copy-done.5
  347.7 2.0 multiply_reduce_fusion.2
  349.7 16.9 %all-reduce.2 = (f32[1]{0:T(128)}, f32[1]{0:T(128)}) all-reduce(f32[1]{0:T(128)} %bitcast.6, f32[1]{0:T(128)} %bitcast.7), channel_id=1, replica_groups=mesh['pipe'=8,'seq'=8,'tensor'=4] {'pipe'}, use_global_device_ids=true, to_apply=%region_10.11 | all-reduce | flops 2 | bytes 16 | tf_op jit(solution)/shard_map/psum | solution.py:51
  (3 shorter events, 0.0 us)
Async XLA Ops:
  6.5 104.4 %copy-start = (bf16[1,3584,32]{1,2,0:T(8,128)(2,1)S(1)}, bf16[1,3584,32]{1,2,0:T(8,128)(2,1)}, u32[]{:S(2)}) copy-start(bf16[1,3584,32]{1,2,0:T(8,128)(2,1)} %param.16) | copy-start | bytes 688132
  6.5 90.8 %all-gather.3.cloned.1.call-start = ((), (), s32[]{:S(2)}) async-start(), calls=%async_computation.4 | async-start | bytes 8257536 | tf_op jit(solution)/shard_map/all_gather | solution.py:13
  7.3 103.4 %copy-start.6 = (s32[32]{0:T(128)S(1)}, s32[32]{0:T(128)}, u32[]{:S(2)}) copy-start(s32[32]{0:T(128)} %param.19) | copy-start | bytes 388
  7.3 134.4 %reduce-scatter.3.cloned.1.call-start = ((), (), s32[]{:S(2)}) async-start(), calls=%async_computation.2 | async-start | bytes 2621440 | tf_op jit(solution)/shard_map/reduce_scatter | solution.py:18
  110.6 81.5 %copy-start.1 = (bf16[256,1024]{1,0:T(8,128)(2,1)S(1)}, bf16[256,1024]{1,0:T(8,128)(2,1)}, u32[]{:S(2)}) copy-start(bf16[256,1024]{1,0:T(8,128)(2,1)} %param.13) | copy-start | bytes 1572868
  110.6 81.5 %copy-start.2 = (bf16[256,1024]{1,0:T(8,128)(2,1)S(1)}, bf16[256,1024]{1,0:T(8,128)(2,1)}, u32[]{:S(2)}) copy-start(bf16[256,1024]{1,0:T(8,128)(2,1)} %param.12) | copy-start | bytes 1572868
  110.6 81.5 %copy-start.3 = (f32[1024]{0:T(1024)S(1)}, f32[1024]{0:T(1024)}, u32[]{:S(2)}) copy-start(f32[1024]{0:T(1024)} %param.14) | copy-start | bytes 12292
  110.6 95.6 %copy-start.7 = (f32[1,1024,32]{1,2,0:T(8,128)S(1)}, f32[1,1024,32]{1,2,0:T(8,128)}, u32[]{:S(2)}) copy-start(f32[1,1024,32]{1,2,0:T(8,128)} %param.15) | copy-start | bytes 393220
  110.6 96.9 %reduce-scatter.5.cloned.1.call-start = ((), (), s32[]{:S(2)}) async-start(), calls=%async_computation.3 | async-start | bytes 163840 | tf_op jit(solution)/shard_map/reduce_scatter | solution.py:35
  116.9 92.8 %copy-start.8 = (u32[256]{0:T(256)S(1)}, u32[256]{0:T(256)}, u32[]{:S(2)}) copy-start(u32[256]{0:T(256)} %constant.28) | copy-start | bytes 3076
  116.9 230.7 %copy-start.4 = (f32[1,1024]{1,0:T(1,128)S(1)}, f32[1,1024]{1,0:T(1,128)}, u32[]{:S(2)}) copy-start(f32[1,1024]{1,0:T(1,128)} %param.17) | copy-start | bytes 12292
  116.9 230.7 %copy-start.5 = (f32[1,1024]{1,0:T(1,128)S(1)}, f32[1,1024]{1,0:T(1,128)}, u32[]{:S(2)}) copy-start(f32[1,1024]{1,0:T(1,128)} %param.18) | copy-start | bytes 12292
  117.0 230.7 %all-reduce.6.cloned.1.call-start = ((), (), s32[]{:S(2)}) async-start(), calls=%async_computation.5 | async-start | bytes 262144
Sparse Core Ops, SparseCore 0:
  9.1 88.1 all-gather.2
  110.7 30.8 reduce-scatter.2
  144.3 20.4 reduce-scatter.4
  209.8 137.8 all-reduce.5
where the time goes:
time: 375 us
  waiting for transfers between devices  253 us (67%)
  blocking collectives  81 us (22%)
  matrix products  21.7 us (6%)
  between operations  15.1 us (4%)
    unnamed x5, waiting for transfers between devices  138 us
    all_gather x1, waiting for transfers between devices, per_device(): gathered = lax.all_gather(hidden[0], 'seq', axis=0, tiled=True)  90 us
    psum x1, blocking collectives, per_device(): summed = lax.psum(partial_value, 'pipe')  50.4 us
    reduce_scatter x1, waiting for transfers between devices, per_device(): lax.psum_scatter(jnp.dot(gathered, weight, preferred_element_type=jnp.flo...  24.6 us
    psum x1, blocking collectives, per_device(): score_total, self_total = lax.psum((score_term, self_term), 'pipe')  16.9 us
    psum x1, blocking collectives, per_device(): lax.psum((jnp.sum(stream * stream, axis=1), jnp.sum(weighted_target * str...  13.7 us
    dot_general x1, matrix products, per_device(): jnp.dot(gathered, weight, preferred_element_type=jnp.float32)  13.3 us
  transfers between devices with their start and end apart: 4, of which 3 were waited for; matrix products, arithmetic and copies ran while one was open for 2% of the time, Pallas kernels for 0%

commit v1 on v0

--- a/solution.py
+++ b/solution.py
@@ -21,7 +21,8 @@
         scatter_dimension=0,
         tiled=True,
     ).astype(jnp.float32)
-    summed = lax.psum(partial_value, "pipe")
+    parts = lax.all_gather(partial_value, "pipe", axis=0, tiled=False)
+    summed = parts.sum(axis=0)
     stream = resid.astype(jnp.float32) + summed
     weighted_target = gain[None, :] * target.astype(jnp.float32)
     square_sum, inner = lax.psum(

time: 375 us -> 389 us (1.037)
  waiting for transfers between devices: 253 us -> 310 us
  blocking collectives: 81 us -> 30.8 us
  other arithmetic: 3.46 us -> 9.97 us
    psum x1 -> x0, blocking collectives: 50.4 us -> none  [per_device(): summed = lax.psum(partial_value, 'pipe')]
    all_gather x0 -> x1, waiting for transfers between devices: none -> 46 us  [per_device(): parts = lax.all_gather(partial_value, 'pipe', axis=0, tiled=False)]
    reduce_scatter x1, waiting for transfers between devices: 24.6 us -> 31 us  [per_device(): lax.psum_scatter(jnp.dot(gathered, weight, preferred_element_type=jnp.flo...]
    reduce_sum x0 -> x1, other arithmetic: none -> 4.38 us  [per_device(): summed = parts.sum(axis=0)]
    unnamed x5 -> x6, waiting for transfers between devices: 138 us -> 140 us
  transfers between devices with their start and end apart: 4 -> 5, of which waited for: 3 -> 5; matrix products, arithmetic and copies ran while one was open for 2% -> 3% of each run, Pallas kernels for 0% -> 0%
where the time goes in v1:
time: 389 us
  waiting for transfers between devices  310 us (80%)
  blocking collectives  30.8 us (8%)
  matrix products  21.7 us (6%)
  between operations  15.2 us (4%)
  other arithmetic  9.97 us (3%)
    unnamed x6, waiting for transfers between devices  140 us
    all_gather x1, waiting for transfers between devices, per_device(): gathered = lax.all_gather(hidden[0], 'seq', axis=0, tiled=True)  90 us
    all_gather x1, waiting for transfers between devices, per_device(): parts = lax.all_gather(partial_value, 'pipe', axis=0, tiled=False)  46 us
    reduce_scatter x1, waiting for transfers between devices, per_device(): lax.psum_scatter(jnp.dot(gathered, weight, preferred_element_type=jnp.flo...  31 us
    psum x1, blocking collectives, per_device(): score_total, self_total = lax.psum((score_term, self_term), 'pipe')  16.9 us
    psum x1, blocking collectives, per_device(): lax.psum((jnp.sum(stream * stream, axis=1), jnp.sum(weighted_target * str...  13.9 us
    dot_general x1, matrix products, per_device(): jnp.dot(gathered, weight, preferred_element_type=jnp.float32)  13.2 us
  transfers between devices with their start and end apart: 5, of which 5 were waited for; matrix products, arithmetic and copies ran while one was open for 3% of the time, Pallas kernels for 0%

profile of v1, /device:TPU:1, one launch (start us, length us, event | category | flops | bytes accessed | tf_op | source)
XLA Modules:
  0.0 388.9 jit_solution(14033356382578409745)
XLA Ops:
  6.5 0.0 copy-start
  6.5 0.0 all-gather.5.cloned.1.call-start
  6.5 0.7 all-gather.5.cloned.1.call-update
  7.3 0.0 copy-start.6
  7.3 0.0 reduce-scatter.3.cloned.1.call-start
  7.3 90.0 %all-gather.5.cloned.1.call-done = bf16[1,1024,3584]{2,1,0:T(8,128)(2,1)} async-done(((bf16[1,128,3584]{2,1,0:T(8,128)(2,1)}), bf16[1,1024,3584]{2,1,0:T(8,128)(2,1)}) %all-gather.5.cloned.1.call-update) | async-done | bytes 7340048 | tf_op jit(solution)/shard_map/all_gather | solution.py:13
  97.3 13.2 %fusion.5 = bf16[1024,1024]{1,0:T(8,128)(2,1)} fusion(bf16[1,3584,1024]{2,1,0:T(8,128)(2,1)} %param.11, bf16[1,1024,3584]{2,1,0:T(8,128)(2,1)} %all-gather.5.cloned.1.call-done), kind=kOutput, calls=%fused_computation.5 | convolution fusion | flops 7517241344 | bytes 16777216 | tf_op jit(solution)/shard_map/dot_general | solution.py:19
  110.5 0.0 reduce-scatter.3.cloned.1.call-update
  110.5 0.0 all-gather.7.cloned.1.call-start
  110.5 31.0 %reduce-scatter.3.cloned.1.call-done = bf16[256,1024]{1,0:T(8,128)(2,1)} async-done(((bf16[1024,1024]{1,0:T(8,128)(2,1)}), bf16[256,1024]{1,0:T(8,128)(2,1)}) %reduce-scatter.3.cloned.1.call-update) | async-done | bytes 524304 | tf_op jit(solution)/shard_map/reduce_scatter | solution.py:18
  141.5 2.2 all_gather.16
  143.7 0.0 all-gather.7.cloned.1.call-update
  143.7 0.0 reduce-scatter.5.cloned.1.call-start
  143.8 0.0 copy-done.6
  143.8 0.1 copy.15
  143.9 0.1 reduce-window.8
  143.9 0.1 reduce.2
  144.1 0.0 copy-done
  144.1 0.0 copy-start.1
  144.1 0.0 copy-start.2
  144.1 0.0 copy-start.3
  144.1 6.0 %fusion.2 = f32[1024,32]{0,1:T(8,128)} fusion(bf16[1,1024,3584]{2,1,0:T(8,128)(2,1)} %all-gather.5.cloned.1.call-done, bf16[1,3584,32]{1,2,0:T(8,128)(2,1)S(1)} %copy-done), kind=kOutput, calls=%fused_computation.2 | convolution fusion | flops 234881024 | bytes 7700480 | tf_op jit(solution)/shard_map/dot_general | solution.py:17
  150.2 0.0 copy-start.7
  150.2 0.0 reduce-scatter.5.cloned.1.call-update
  150.2 0.0 all-reduce.5.cloned.1.call-start
  150.2 46.0 %all-gather.7.cloned.1.call-done = f32[2048,1024]{1,0:T(8,128)} async-done(((f32[256,1024]{1,0:T(8,128)}), f32[2048,1024]{1,0:T(8,128)}) %all-gather.7.cloned.1.call-update) | async-done | bytes 8388624 | tf_op jit(solution)/shard_map/all_gather | solution.py:24
  196.2 0.0 copy-start.8
  196.2 0.0 copy-start.4
  196.2 0.0 copy-start.5
  196.2 4.4 %reduce_sum.49 = f32[256,1024]{1,0:T(8,128)S(1)} reduce(f32[8,256,1024]{2,1,0:T(8,128)} %bitcast.25, f32[]{:T(128)} %constant.7.clone.1), dimensions={0}, to_apply=%region_2.0 | reduce | flops 1835008 | bytes 9437188 | tf_op jit(solution)/shard_map/reduce_sum | solution.py:25
  200.6 0.0 copy-done.1
  200.6 0.0 copy-done.2
  200.6 0.0 copy-done.3
  200.6 0.4 multiply_reduce_fusion.1
  201.0 13.9 %all-reduce.1 = (f32[256]{0:T(256)S(1)}, f32[256]{0:T(256)S(1)}) all-reduce(f32[256]{0:T(256)S(1)} %get-tuple-element.6, f32[256]{0:T(256)S(1)} %get-tuple-element.5), channel_id=1, replica_groups=mesh['pipe'=8,'seq'=8,'tensor'=4] {'seq'}, use_global_device_ids=true, to_apply=%region_6.0 | all-reduce | flops 512 | bytes 4096 | tf_op jit(solution)/shard_map/psum | solution.py:28
  214.9 0.0 copy-done.7
  214.9 1.2 fusion.10
  216.1 3.4 reduce-scatter.5.cloned.1.call-done
  219.5 0.9 broadcast_multiply_fusion
  220.3 1.3 fusion.19
  221.6 0.0 all-reduce.5.cloned.1.call-update
  221.7 0.0 copy-done.8
  221.7 0.6 dynamic-slice
  222.3 139.3 %all-reduce.5.cloned.1.call-done = f32[32,1024]{1,0:T(8,128)} async-done(((f32[32,1024]{1,0:T(8,128)}), f32[32,1024]{1,0:T(8,128)}) %all-reduce.5.cloned.1.call-update) | async-done | bytes 131088
  361.6 0.0 copy-done.4
  361.6 0.0 copy-done.5
  361.6 2.0 multiply_reduce_fusion.2
  363.6 16.9 %all-reduce.2 = (f32[1]{0:T(128)}, f32[1]{0:T(128)}) all-reduce(f32[1]{0:T(128)} %bitcast.7, f32[1]{0:T(128)} %bitcast.8), channel_id=1, replica_groups=mesh['pipe'=8,'seq'=8,'tensor'=4] {'pipe'}, use_global_device_ids=true, to_apply=%region_10.11 | all-reduce | flops 2 | bytes 16 | tf_op jit(solution)/shard_map/psum | solution.py:52
  (3 shorter events, 0.0 us)
Async XLA Ops:
  6.5 137.5 %copy-start = (bf16[1,3584,32]{1,2,0:T(8,128)(2,1)S(1)}, bf16[1,3584,32]{1,2,0:T(8,128)(2,1)}, u32[]{:S(2)}) copy-start(bf16[1,3584,32]{1,2,0:T(8,128)(2,1)} %param.16) | copy-start | bytes 688132
  6.5 90.8 %all-gather.5.cloned.1.call-start = ((), (), s32[]{:S(2)}) async-start(), calls=%async_computation.4 | async-start | bytes 8257536 | tf_op jit(solution)/shard_map/all_gather | solution.py:13
  7.3 136.5 %copy-start.6 = (s32[32]{0:T(128)S(1)}, s32[32]{0:T(128)}, u32[]{:S(2)}) copy-start(s32[32]{0:T(128)} %param.19) | copy-start | bytes 388
  7.3 134.3 %reduce-scatter.3.cloned.1.call-start = ((), (), s32[]{:S(2)}) async-start(), calls=%async_computation.2 | async-start | bytes 2621440 | tf_op jit(solution)/shard_map/reduce_scatter | solution.py:18
  110.5 85.7 %all-gather.7.cloned.1.call-start = ((), (), s32[]{:S(2)}) async-start(), calls=%async_computation.5 | async-start | bytes 9437184 | tf_op jit(solution)/shard_map/all_gather | solution.py:24
  143.7 75.7 %reduce-scatter.5.cloned.1.call-start = ((), (), s32[]{:S(2)}) async-start(), calls=%async_computation.3 | async-start | bytes 163840 | tf_op jit(solution)/shard_map/reduce_scatter | solution.py:36
  144.1 56.5 %copy-start.1 = (bf16[256,1024]{1,0:T(8,128)(2,1)S(1)}, bf16[256,1024]{1,0:T(8,128)(2,1)}, u32[]{:S(2)}) copy-start(bf16[256,1024]{1,0:T(8,128)(2,1)} %param.13) | copy-start | bytes 1572868
  144.1 56.5 %copy-start.2 = (bf16[256,1024]{1,0:T(8,128)(2,1)S(1)}, bf16[256,1024]{1,0:T(8,128)(2,1)}, u32[]{:S(2)}) copy-start(bf16[256,1024]{1,0:T(8,128)(2,1)} %param.12) | copy-start | bytes 1572868
  144.1 56.5 %copy-start.3 = (f32[1024]{0:T(1024)S(1)}, f32[1024]{0:T(1024)}, u32[]{:S(2)}) copy-start(f32[1024]{0:T(1024)} %param.14) | copy-start | bytes 12292
  150.2 64.7 %copy-start.7 = (f32[1,1024,32]{1,2,0:T(8,128)S(1)}, f32[1,1024,32]{1,2,0:T(8,128)}, u32[]{:S(2)}) copy-start(f32[1,1024,32]{1,2,0:T(8,128)} %param.15) | copy-start | bytes 393220
  150.2 211.4 %all-reduce.5.cloned.1.call-start = ((), (), s32[]{:S(2)}) async-start(), calls=%async_computation.6 | async-start | bytes 262144
  196.2 25.5 %copy-start.8 = (u32[256]{0:T(256)S(1)}, u32[256]{0:T(256)}, u32[]{:S(2)}) copy-start(u32[256]{0:T(256)} %constant.28) | copy-start | bytes 3076
  196.2 165.4 %copy-start.4 = (f32[1,1024]{1,0:T(1,128)S(1)}, f32[1,1024]{1,0:T(1,128)}, u32[]{:S(2)}) copy-start(f32[1,1024]{1,0:T(1,128)} %param.17) | copy-start | bytes 12292
  196.2 165.4 %copy-start.5 = (f32[1,1024]{1,0:T(1,128)S(1)}, f32[1,1024]{1,0:T(1,128)}, u32[]{:S(2)}) copy-start(f32[1,1024]{1,0:T(1,128)} %param.18) | copy-start | bytes 12292
Sparse Core Ops, SparseCore 0:
  9.1 88.0 all-gather.4
  110.6 30.9 reduce-scatter.2
  143.8 52.3 all-gather.6
  198.7 20.7 reduce-scatter.4
  222.8 138.7 all-reduce.4
